TPU v7x, 512 devices: a whole 4x4x16 slice. The times are simulated.
512 devices in a mesh: space: 32 (over z_lo, x, core), species: 16 (over y, z_hi).
Axes of the slice: x: 4, y: 4, z: 16 (z_hi: 4, z_lo: 4; z = z_hi * 4 + z_lo), core: 2. Of those that a mesh axis runs over, the one named last changes fastest.
Arguments:
- biomass: bfloat16 [512, 64, 1024], P('species', 'space'), may hold values from 0.019897461 to 1
- resources: float32 [128, 64, 1024], P('species', 'space'), may hold values from 0.1 to 4
- capacity: float32 [512, 128], P('species'), may hold values from 0.002 to 0.05
- affinity: float32 [512, 128], P('species'), may hold values from 0.2 to 5
- secretion: bfloat16 [128, 512], P(None, 'species'), may hold values from 0 to 0.059814453
- energy_yield: float32 [128], replicated, may hold values from 0.5 to 2
- maintenance: float32 [512], P('species'), may hold values from 0.3 to 3
- motility: float32 [512], P('species'), may hold values from 0.04 to 0.6
- diffusivity: float32 [128], P('species'), may hold values from 0.02 to 0.6
- supply: float32 [128], P('species'), may hold values from 0.4 to 4
Outputs:
- growth: float32 [512, 64, 1024], P('species', 'space')
- new_biomass: float32 [512, 64, 1024], P('species', 'space')
- new_resources: float32 [128, 64, 1024], P('species', 'space')
All inputs are finite; a program needn't handle non-finite values.
Results may differ from a plain program's by a relative error of at most 0.0003.
Values may be sent and summed in bfloat16 or wider, within the bound.
A program may use at most 64 MiB of HBM per device.

v0:
```python
import math
import jax
import jax.numpy as jnp
from jax import lax
from jax.sharding import PartitionSpec as P

NY = 16
NZ = 64
time_step = 0.25


def extended_2(block, sides, width):
    for axis, dim in sides:
        count = lax.axis_size(axis)
        forward = [(i, i + 1) for i in range(count - 1)]
        forward.append((count - 1, 0))
        backward = [(target, source) for source, target in forward]
        low = lax.ppermute(
            lax.slice_in_dim(block, block.shape[dim] - width, None, axis=dim), axis, forward
        )
        high = lax.ppermute(lax.slice_in_dim(block, 0, width, axis=dim), axis, backward)
        block = jnp.concatenate([low, block, high], axis=dim)
    return block


def laplace(padded, depth_cells, width_cells):
    channel_count = padded.shape[0]
    inner_cells = padded[:, 1:-1, :]
    slab_rows = inner_cells.shape[1]
    block_view = inner_cells.reshape(channel_count, slab_rows, depth_cells, width_cells)
    extended = jnp.pad(block_view, ((0, 0), (0, 0), (1, 1), (1, 1)), mode="edge")
    beside_x = padded[:, 2:, :] + padded[:, :-2, :]
    beside_yz = (
        extended[:, :, 2:, 1:-1]
        + extended[:, :, :-2, 1:-1]
        + extended[:, :, 1:-1, 2:]
        + extended[:, :, 1:-1, :-2]
    )
    return beside_x + beside_yz.reshape(channel_count, slab_rows, -1) - 6.0 * inner_cells


def spread_biomass(biomass, motility):
    padded = extended_2(biomass, (("space", 1),), 1).astype(jnp.float32)
    return motility[:, None, None] * laplace(padded, NY, NZ)


def spread_resources(resources, diffusivity):
    padded = extended_2(resources, (("space", 1),), 1)
    return diffusivity[:, None, None] * laplace(padded, NY, NZ)


def per_device(
    biomass,
    resources,
    capacity,
    affinity,
    secretion,
    energy_yield,
    maintenance,
    motility,
    diffusivity,
    supply,
):
    local_strains, slab_rows, plane_cells = biomass.shape
    cells_dev = slab_rows * plane_cells
    seen = lax.all_gather(resources.astype(jnp.bfloat16), "species", axis=0, tiled=True)
    all_resources = seen.shape[0]
    seen_flat = seen.reshape(all_resources, cells_dev)
    mass_flat = biomass.reshape(local_strains, cells_dev)
    block_cells = math.gcd(256, cells_dev)
    block_count = cells_dev // block_cells

    def per_block(block_index, carry):
        growth_all, consumed_all, secreted_all = carry
        start = block_index * block_cells
        seen_block = lax.dynamic_slice_in_dim(seen_flat, start, block_cells, 1).astype(jnp.float32)
        mass_block = lax.dynamic_slice_in_dim(mass_flat, start, block_cells, 1).astype(jnp.float32)
        uptake = (
            capacity[:, :, None]
            * seen_block[None, :, :]
            / (affinity[:, :, None] + seen_block[None, :, :])
        )
        growth_block = jnp.sum(energy_yield[None, :, None] * uptake, axis=1) - maintenance[:, None]
        flux_block = jnp.sum(uptake, axis=1)
        product_block = (mass_block * flux_block).astype(jnp.bfloat16)
        consumed_block = jnp.sum(mass_block[:, None, :] * uptake, axis=0)
        secreted_block = jnp.dot(secretion, product_block, preferred_element_type=jnp.float32)
        growth_all = lax.dynamic_update_slice_in_dim(growth_all, growth_block, start, 1)
        consumed_all = lax.dynamic_update_slice_in_dim(consumed_all, consumed_block, start, 1)
        secreted_all = lax.dynamic_update_slice_in_dim(secreted_all, secreted_block, start, 1)
        return (growth_all, consumed_all, secreted_all)

    initial = (
        jnp.zeros((local_strains, cells_dev), jnp.float32),
        jnp.zeros((all_resources, cells_dev), jnp.float32),
        jnp.zeros((all_resources, cells_dev), jnp.float32),
    )
    growth_all, consumed_all, secreted_all = lax.fori_loop(0, block_count, per_block, initial)
    growth = growth_all.reshape(local_strains, slab_rows, plane_cells)
    consumed_all = consumed_all.reshape(all_resources, slab_rows, plane_cells)
    secreted_all = secreted_all.reshape(all_resources, slab_rows, plane_cells)
    consumed_owned, secreted_owned = (
        lax.psum_scatter(consumed_all, "species", scatter_dimension=0, tiled=True),
        lax.psum_scatter(secreted_all, "species", scatter_dimension=0, tiled=True),
    )
    net_owned = secreted_owned - consumed_owned
    mass_spread = spread_biomass(biomass, motility)
    resource_spread = spread_resources(resources, diffusivity)
    mass = biomass.astype(jnp.float32)
    new_biomass = mass + time_step * (mass * growth + mass_spread)
    new_resources = resources + time_step * (resource_spread + net_owned + supply[:, None, None])
    return (growth, new_biomass, new_resources)


def solution(mesh):
    return jax.shard_map(
        per_device,
        mesh=mesh,
        in_specs=(
            P("species", "space", None),
            P("species", "space", None),
            P("species", None),
            P("species", None),
            P(None, "species"),
            P(),
            P("species"),
            P("species"),
            P("species"),
            P("species"),
        ),
        out_specs=(
            P("species", "space", None),
            P("species", "space", None),
            P("species", "space", None),
        ),
        check_vma=False,
    )
```

profile of v0, /device:TPU:78, one launch (start us, length us, event | category | flops | bytes accessed | tf_op | source)
XLA Modules:
  0.0 375.8 jit_solution(9521856368249420357)
XLA Ops:
  7.2 0.9 convert_element_type.30
  8.1 57.8 %all_gather.3 = bf16[128,2,1024]{2,1,0:T(2,128)(2,1)S(1)} all-gather(bf16[8,2,1024]{2,1,0:T(2,128)(2,1)S(1)} %convert_element_type.30), channel_id=1, replica_groups=mesh['space'=32,'species'=16] {'species'}, dimensions={0}, use_global_device_ids=true | all-gather | bytes 557056 | tf_op jit(solution)/shard_map/all_gather | solution.py:66
  66.4 0.5 copy-done.3
  66.9 20.4 %while.17 = (s32[]{:T(128)}, f32[32,2048]{1,0:T(8,128)S(1)}, f32[128,2048]{1,0:T(8,128)S(1)}, f32[128,2048]{0,1:T(8,128)S(1)}, f32[128]{0:T(128)S(1)}, /*index=5...) while((s32[]{:T(128)}, f32[32,2048]{1,0:T(8,128)S(1)}, ...), condition=%wide.region_4.0_spmd, body=%wide.region_0.0_spmd.sunk | while | flops 10510342 | bytes 1157331 | solution.py:98
  66.9 2.2 fusion.32
  69.5 2.2 fusion.32
  72.0 2.2 fusion.32
  74.6 2.2 fusion.32
  77.1 2.2 fusion.32
  79.7 2.2 fusion.32
  82.2 2.2 fusion.32
  84.8 2.2 fusion.32
  87.3 1.9 reshape.50
  89.1 1.3 copy.19
  90.7 1.9 collective-permute-start.1
  92.6 2.4 collective-permute-start
  95.1 1.9 collective-permute-start.3
  97.0 3.6 collective-permute-start.2
  101.6 1.3 dynamic-slice
  103.5 0.4 maximum_convert_fusion
  104.9 0.7 fusion.3
  105.9 1.2 convert_add_fusion
  107.1 260.1 %all-reduce.5.cloned.1.call-done = (f32[128,2,1024]{2,1,0:T(2,128)}, f32[128,2,1024]{2,1,0:T(2,128)}) async-done(((f32[128,2,1024]{2,1,0:T(2,128)}, f32[128,2,1024]{2,1,0:T(2,128)}), (f32[128,2,1024]{2,1,0:T(2,128)}, f32[128,2,1024]{2,1,0:T(2,128)})) %all-reduce.5.cloned.1.call-update) | async-done | bytes 2097168
  367.2 1.7 fusion.20
  (87 shorter events, 5.3 us)
Async XLA Ops:
  7.2 58.9 %copy-start = (bf16[32,2,1024]{2,1,0:T(2,128)(2,1)S(1)}, bf16[32,2,1024]{2,1,0:T(2,128)(2,1)}, u32[]{:S(2)}) copy-start(bf16[32,2,1024]{2,1,0:T(2,128)(2,1)} %param.12) | copy-start | bytes 393220
  7.2 360.0 %all-reduce.5.cloned.1.call-start = ((), (), s32[]{:S(2)}) async-start(), calls=%async_computation | async-start | bytes 4194304
  66.1 0.7 copy-start.3
  66.1 0.7 copy-start.4
  66.1 0.7 copy-start.5
  66.1 0.7 copy-start.6
  66.2 0.7 copy-start.7
  90.5 4.6 %copy-start.2 = (f32[8,2,1024]{2,1,0:T(2,128)S(1)}, f32[8,2,1024]{2,1,0:T(2,128)}, u32[]{:S(2)}) copy-start(f32[8,2,1024]{2,1,0:T(2,128)} %param.13) | copy-start | bytes 196612
  90.7 12.8 %collective-permute-start.1 = (bf16[32,1,1024]{2,1,0:T(2,128)(2,1)S(1)}, bf16[32,1,1024]{2,1,0:T(2,128)(2,1)S(1)}, u32[]{:S(2)}, u32[]{:S(2)}) collective-permute-start(bf16[32,1,1024]{2,1,0:T(2,128)(2,1)S(1)} %get-tuple-element.261), channel_id=1, source_target_pairs={{16,0},{32,16},{48,32},{64,48},{80,64},{96,80},{112,96},{128,112},... | collective-permute-start | bytes 196616 | tf_op jit(solution)/shard_map/ppermute | solution.py:21
  92.6 10.9 %collective-permute-start = (bf16[32,1,1024]{2,1,0:T(2,128)(2,1)S(1)}, bf16[32,1,1024]{2,1,0:T(2,128)(2,1)S(1)}, u32[]{:S(2)}, u32[]{:S(2)}) collective-permute-start(bf16[32,1,1024]{2,1,0:T(2,128)(2,1)S(1)} %get-tuple-element.260), channel_id=1, source_target_pairs={{0,16},{16,32},{32,48},{48,64},{64,80},{80,96},{96,112},{112,128},... | collective-permute-start | bytes 196616 | tf_op jit(solution)/shard_map/ppermute | solution.py:18
  95.1 12.0 %collective-permute-start.3 = (f32[8,1,1024]{2,1,0:T(1,128)S(1)}, f32[8,1,1024]{2,1,0:T(1,128)S(1)}, u32[]{:S(2)}, u32[]{:S(2)}) collective-permute-start(f32[8,1,1024]{2,1,0:T(1,128)S(1)} %get-tuple-element.263), channel_id=1, source_target_pairs={{0,16},{16,32},{32,48},{48,64},{64,80},{80,96},{96,112},{112,128},... | collective-permute-start | bytes 98312 | tf_op jit(solution)/shard_map/ppermute | solution.py:18
  97.0 10.1 %collective-permute-start.2 = (f32[8,1,1024]{2,1,0:T(1,128)S(1)}, f32[8,1,1024]{2,1,0:T(1,128)S(1)}, u32[]{:S(2)}, u32[]{:S(2)}) collective-permute-start(f32[8,1,1024]{2,1,0:T(1,128)S(1)} %get-tuple-element.262), channel_id=1, source_target_pairs={{16,0},{32,16},{48,32},{64,48},{80,64},{96,80},{112,96},{128,112},... | collective-permute-start | bytes 98312 | tf_op jit(solution)/shard_map/ppermute | solution.py:21
  101.0 4.8 %copy-start.1 = (f32[32,2,1024]{2,1,0:T(2,128)}, f32[32,2,1024]{2,1,0:T(2,128)S(1)}, u32[]{:S(2)}) copy-start(f32[32,2,1024]{2,1,0:T(2,128)S(1)} %reshape.44) | copy-start | bytes 786436
  104.9 0.9 copy-start.8
  105.8 261.4 %copy-start.9 = (f32[8]{0:T(128)S(1)}, f32[8]{0:T(128)}, u32[]{:S(2)}) copy-start(f32[8]{0:T(128)} %param.21) | copy-start | bytes 100
  105.9 261.4 %copy-start.10 = (f32[8]{0:T(128)S(1)}, f32[8]{0:T(128)}, u32[]{:S(2)}) copy-start(f32[8]{0:T(128)} %param.20) | copy-start | bytes 100
Sparse Core Ops, SparseCore 0:
  90.6 276.5 all-reduce.4
where the time goes:
time: 376 us
  waiting for transfers between devices  260 us (69%)
  blocking collectives  57.8 us (15%)
  other arithmetic  23.6 us (6%)
  between operations  15 us (4%)
  starting transfers between devices  9.93 us (3%)
  local copies, waits for them, and re-layouts  7.3 us (2%)
    unnamed x2, waiting for transfers between devices  260 us
    all_gather x1, blocking collectives, per_device(): lax.all_gather(resources.astype(jnp.bfloat16), 'species', axis=0, tiled=T...  57.8 us
    reduce_sum x8, other arithmetic, per_block(): flux_block = jnp.sum(uptake, axis=1)  17.5 us
  transfers between devices with their start and end apart: 5, of which 1 were waited for; matrix products, arithmetic and copies ran while one was open for 2% of the time, Pallas kernels for 0%

commit v1 on v0

--- a/solution.py
+++ b/solution.py
@@ -1,12 +1,30 @@
+import functools
 import math
 import jax
 import jax.numpy as jnp
 from jax import lax
 from jax.sharding import PartitionSpec as P
+from jax.lax import all_to_all, axis_size
 
 NY = 16
 NZ = 64
 time_step = 0.25
+
+
+def target_press(sample, dim_at):
+    current_value = jnp.concatenate(
+        all_to_all(
+            jnp.stack([sample for _ in range(axis_size("species"))], axis=0),
+            axis_name="species",
+            split_axis=0,
+            concat_axis=0,
+        ),
+        axis=dim_at,
+    )
+    return current_value
+
+
+load_sections_in = functools.partial(target_press, dim_at=0)
 
 
 def extended_2(block, sides, width):
@@ -63,7 +81,7 @@
 ):
     local_strains, slab_rows, plane_cells = biomass.shape
     cells_dev = slab_rows * plane_cells
-    seen = lax.all_gather(resources.astype(jnp.bfloat16), "species", axis=0, tiled=True)
+    seen = load_sections_in(resources.astype(jnp.bfloat16))
     all_resources = seen.shape[0]
     seen_flat = seen.reshape(all_resources, cells_dev)
     mass_flat = biomass.reshape(local_strains, cells_dev)

time: 376 us -> 360 us (0.957)
  blocking collectives: 57.8 us -> 0 us
  waiting for transfers between devices: 260 us -> 284 us
  starting transfers between devices: 9.93 us -> 26.3 us
    all_gather x1 -> x0, blocking collectives: 57.8 us -> none  [per_device(): lax.all_gather(resources.astype(jnp.bfloat16), 'species', axis=0, tiled=T...]
    all_to_all x0 -> x1, waiting for transfers between devices: none -> 32.6 us  [target_press(): all_to_all(jnp.stack([sample for _ in range(axis_size('species'))], axis=...]
    all_to_all x0 -> x1, starting transfers between devices: none -> 16.4 us  [target_press(): all_to_all(jnp.stack([sample for _ in range(axis_size('species'))], axis=...]
    unnamed x2, waiting for transfers between devices: 260 us -> 251 us
  transfers between devices with their start and end apart: 5 -> 6, of which waited for: 1 -> 2; matrix products, arithmetic and copies ran while one was open for 2% -> 2% of each run, Pallas kernels for 0% -> 0%
where the time goes in v1:
time: 360 us; the launch traced here: 359 us
  waiting for transfers between devices  284 us (79%)
  starting transfers between devices  26.3 us (7%)
  other arithmetic  23.6 us (7%)
  between operations  15 us (4%)
  local copies, waits for them, and re-layouts  8.18 us (2%)
    unnamed x2, waiting for transfers between devices  251 us
    all_to_all x1, waiting for transfers between devices, target_press(): all_to_all(jnp.stack([sample for _ in range(axis_size('species'))], axis=...  32.6 us
    reduce_sum x8, other arithmetic, per_block(): flux_block = jnp.sum(uptake, axis=1)  17.5 us
    all_to_all x1, starting transfers between devices, target_press(): all_to_all(jnp.stack([sample for _ in range(axis_size('species'))], axis=...  16.4 us
  transfers between devices with their start and end apart: 6, of which 2 were waited for; matrix products, arithmetic and copies ran while one was open for 2% of the time, Pallas kernels for 0%

profile of v1, /device:TPU:78, one launch (start us, length us, event | category | flops | bytes accessed | tf_op | source)
XLA Modules:
  0.0 359.1 jit_solution(3247437523294100946)
XLA Ops:
  7.2 0.9 convert_element_type.30
  8.1 0.9 stack.2
  9.0 16.4 %all-to-all-start = ((bf16[16,8,2,1024]{3,1,2,0:T(8,128)(2,1)}), bf16[16,8,2,1024]{3,1,2,0:T(8,128)(2,1)S(1)}, u32[]{:S(2)}, u32[]{:S(2)}) async-start(bf16[16,8,2,1024]{3,1,2,0:T(8,128)(2,1)} %stack.2), calls=%async_computation | async-start | bytes 1048576 | tf_op jit(solution)/shard_map/all_to_all | solution.py:16
  25.4 32.6 %all-to-all-done = bf16[16,8,2,1024]{3,1,2,0:T(8,128)(2,1)S(1)} async-done(((bf16[16,8,2,1024]{3,1,2,0:T(8,128)(2,1)}), bf16[16,8,2,1024]{3,1,2,0:T(8,128)(2,1)S(1)}, u32[]{:S(2)}, u32[]{:S(2)}) %all-to-all-start) | async-done | bytes 524320 | tf_op jit(solution)/shard_map/all_to_all | solution.py:16
  58.8 20.4 %while.17 = (s32[]{:T(128)}, f32[32,2048]{1,0:T(8,128)S(1)}, f32[128,2048]{1,0:T(8,128)S(1)}, f32[128,2048]{0,1:T(8,128)S(1)}, f32[128]{0:T(128)S(1)}, /*index=5...) while((s32[]{:T(128)}, f32[32,2048]{1,0:T(8,128)S(1)}, ...), condition=%wide.region_4.0_spmd, body=%wide.region_0.0_spmd.sunk | while | flops 10510342 | bytes 1157331 | solution.py:116
  58.9 2.2 fusion.32
  61.4 2.2 fusion.32
  64.0 2.2 fusion.32
  66.5 2.2 fusion.32
  69.1 2.2 fusion.32
  71.6 2.2 fusion.32
  74.2 2.2 fusion.32
  76.8 2.2 fusion.32
  79.2 1.9 reshape.48
  81.1 1.3 copy.22
  82.6 1.9 collective-permute-start.1
  84.6 2.4 collective-permute-start
  87.1 3.1 collective-permute-start.3
  90.2 2.5 collective-permute-start.2
  93.3 1.3 dynamic-slice
  96.6 0.7 fusion.3
  97.9 1.2 convert_add_fusion
  99.1 251.4 %all-reduce.5.cloned.1.call-done = (f32[128,2,1024]{2,1,0:T(2,128)}, f32[128,2,1024]{2,1,0:T(2,128)}) async-done(((f32[128,2,1024]{2,1,0:T(2,128)}, f32[128,2,1024]{2,1,0:T(2,128)}), (f32[128,2,1024]{2,1,0:T(2,128)}, f32[128,2,1024]{2,1,0:T(2,128)})) %all-reduce.5.cloned.1.call-update) | async-done | bytes 2097168
  350.6 1.7 fusion.20
  (89 shorter events, 6.2 us)
Async XLA Ops:
  7.2 18.2 %copy-start = (bf16[32,2,1024]{2,1,0:T(2,128)(2,1)S(1)}, bf16[32,2,1024]{2,1,0:T(2,128)(2,1)}, u32[]{:S(2)}) copy-start(bf16[32,2,1024]{2,1,0:T(2,128)(2,1)} %param.12) | copy-start | bytes 393220
  9.0 49.1 %all-to-all-start = ((bf16[16,8,2,1024]{3,1,2,0:T(8,128)(2,1)}), bf16[16,8,2,1024]{3,1,2,0:T(8,128)(2,1)S(1)}, u32[]{:S(2)}, u32[]{:S(2)}) async-start(bf16[16,8,2,1024]{3,1,2,0:T(8,128)(2,1)} %stack.2), calls=%async_computation | async-start | bytes 1048576 | tf_op jit(solution)/shard_map/all_to_all | solution.py:16
  25.3 325.2 %all-reduce.5.cloned.1.call-start = ((), (), s32[]{:S(2)}) async-start(), calls=%async_computation.1 | async-start | bytes 4194304
  58.1 0.7 copy-start.3
  58.1 0.7 copy-start.4
  58.1 0.7 copy-start.5
  58.1 0.7 copy-start.6
  58.1 0.7 copy-start.7
  82.4 4.6 %copy-start.2 = (f32[8,2,1024]{2,1,0:T(2,128)S(1)}, f32[8,2,1024]{2,1,0:T(2,128)}, u32[]{:S(2)}) copy-start(f32[8,2,1024]{2,1,0:T(2,128)} %param.13) | copy-start | bytes 196612
  82.6 12.6 %collective-permute-start.1 = (bf16[32,1,1024]{2,1,0:T(2,128)(2,1)S(1)}, bf16[32,1,1024]{2,1,0:T(2,128)(2,1)S(1)}, u32[]{:S(2)}, u32[]{:S(2)}) collective-permute-start(bf16[32,1,1024]{2,1,0:T(2,128)(2,1)S(1)} %get-tuple-element.261), channel_id=1, source_target_pairs={{16,0},{32,16},{48,32},{64,48},{80,64},{96,80},{112,96},{128,112},... | collective-permute-start | bytes 196616 | tf_op jit(solution)/shard_map/ppermute | solution.py:39
  84.6 10.7 %collective-permute-start = (bf16[32,1,1024]{2,1,0:T(2,128)(2,1)S(1)}, bf16[32,1,1024]{2,1,0:T(2,128)(2,1)S(1)}, u32[]{:S(2)}, u32[]{:S(2)}) collective-permute-start(bf16[32,1,1024]{2,1,0:T(2,128)(2,1)S(1)} %get-tuple-element.260), channel_id=1, source_target_pairs={{0,16},{16,32},{32,48},{48,64},{64,80},{80,96},{96,112},{112,128},... | collective-permute-start | bytes 196616 | tf_op jit(solution)/shard_map/ppermute | solution.py:36
  87.1 12.1 %collective-permute-start.3 = (f32[8,1,1024]{2,1,0:T(1,128)S(1)}, f32[8,1,1024]{2,1,0:T(1,128)S(1)}, u32[]{:S(2)}, u32[]{:S(2)}) collective-permute-start(f32[8,1,1024]{2,1,0:T(1,128)S(1)} %get-tuple-element.263), channel_id=1, source_target_pairs={{0,16},{16,32},{32,48},{48,64},{64,80},{80,96},{96,112},{112,128},... | collective-permute-start | bytes 98312 | tf_op jit(solution)/shard_map/ppermute | solution.py:36
  90.2 9.0 %collective-permute-start.2 = (f32[8,1,1024]{2,1,0:T(1,128)S(1)}, f32[8,1,1024]{2,1,0:T(1,128)S(1)}, u32[]{:S(2)}, u32[]{:S(2)}) collective-permute-start(f32[8,1,1024]{2,1,0:T(1,128)S(1)} %get-tuple-element.262), channel_id=1, source_target_pairs={{16,0},{32,16},{48,32},{64,48},{80,64},{96,80},{112,96},{128,112},... | collective-permute-start | bytes 98312 | tf_op jit(solution)/shard_map/ppermute | solution.py:39
  97.3 0.7 copy-start.8
  97.6 253.0 %copy-start.9 = (f32[8]{0:T(128)S(1)}, f32[8]{0:T(128)}, u32[]{:S(2)}) copy-start(f32[8]{0:T(128)} %param.21) | copy-start | bytes 100
  97.6 253.0 %copy-start.10 = (f32[8]{0:T(128)S(1)}, f32[8]{0:T(128)}, u32[]{:S(2)}) copy-start(f32[8]{0:T(128)} %param.20) | copy-start | bytes 100
  97.9 254.4 %copy-start.1 = (f32[32,2,1024]{2,1,0:T(2,128)}, f32[32,2,1024]{2,1,0:T(2,128)S(1)}, u32[]{:S(2)}) copy-start(f32[32,2,1024]{2,1,0:T(2,128)S(1)} %reshape.42) | copy-start | bytes 786436
Sparse Core Ops, SparseCore 0:
  82.6 267.9 all-reduce.4
